TPU v7x, 128 devices: a whole 4x4x4 slice. The times are simulated.
128 devices in a mesh: vel: 32 (over x_hi, y, z), space: 4 (over x_lo, core).
Axes of the slice: x: 4 (x_hi: 2, x_lo: 2; x = x_hi * 2 + x_lo), y: 4, z: 4, core: 2. Of those that a mesh axis runs over, the one named last changes fastest.
Arguments:
- dist: float32 [4096, 32, 1024], P('vel', 'space'), may hold values from -6 to 6
- vel_index: int32 [3, 4096], P(None, 'vel'), may hold values from 0 to 15, as said below
- relax: float32 [32, 1024], P('space'), may hold values from 0.05 to 0.9
- wall_mask: int32 [32, 1024], P('space'), may hold values 0 or 1
- macro_inverse: float32 [13, 13], replicated, may hold values from -1.5 to 1.5
Outputs:
- dist_out: float32 [4096, 32, 1024], P('vel', 'space')
- macro_fields: float32 [13, 32, 1024], P(None, 'space', 'vel')
- change_norm: float32 [2], replicated
Inputs may be any that keep to these rules, and one draw needn't show every extreme that they name: `vel_index`: each point of the velocity grid of 4096 points appears in exactly one column.
All inputs are finite; a program needn't handle non-finite values. No bound on the sum of `wall_mask` on one device may be relied on, other than what follows from the above.
Results may differ from a plain program's by a relative error of at most 0.0003.
Values sent between devices are 32-bit elements; how exact they have to be, the bound alone decides.
A program may use at most 128 MiB of HBM per device.

v0:
```python
import math
import jax
import jax.numpy as jnp
from jax import lax
from jax.sharding import PartitionSpec as P

NVX = 16
NY = 64
NZ = 16
MOM = 13
SWEEPS = 3
ITERS = 2
speed_range = 4.0
time_step = 0.08
coupling = 0.5


def with_halo(shard, sides, width):
    for axis, dim in sides:
        peers, length = (lax.axis_size(axis), shard.shape[dim])
        up = [(i, (i + 1) % peers) for i in range(peers)]
        down = [(j, i) for i, j in up]
        last = lax.slice_in_dim(shard, length - width, length, axis=dim)
        first = lax.slice_in_dim(shard, 0, width, axis=dim)
        before = lax.ppermute(last, axis, up)
        after = lax.ppermute(first, axis, down)
        shard = jnp.concatenate([before, shard, after], axis=dim)
    return shard


def velocities(vel_index):
    return speed_range * (2.0 * vel_index.astype(jnp.float32) + 1.0 - NVX) / NVX


def bases(velocity):
    cxv, cyv, czv = (velocity[0], velocity[1], velocity[2])
    square = cxv * cxv + cyv * cyv + czv * czv
    weights = (2.0 * speed_range / NVX) ** 3 * math.pi ** (-1.5) * jnp.exp(-square)
    heat = square - 2.5
    functions = jnp.stack(
        [
            jnp.ones_like(cxv),
            cxv,
            cyv,
            czv,
            2.0 * square / 3.0 - 1.0,
            2.0 * cxv * cyv,
            2.0 * cxv * czv,
            2.0 * cyv * czv,
            cxv * cxv - cyv * cyv,
            cyv * cyv - czv * czv,
            cxv * heat,
            cyv * heat,
            czv * heat,
        ],
        0,
    )
    moment_rows = functions * weights[None, :]
    factor = 4.0 / 15.0
    shakhov = jnp.stack(
        [
            jnp.ones_like(cxv),
            2.0 * cxv,
            2.0 * cyv,
            2.0 * czv,
            square - 1.5,
            factor * cxv * heat,
            factor * cyv * heat,
            factor * czv * heat,
        ],
        1,
    )
    walls = jnp.stack([jnp.ones_like(cxv), square - 1.5], 1)
    return (moment_rows, shakhov, walls)


def upwind_local(block, speed, axis):
    lower = jnp.roll(block, 1, axis)
    higher = jnp.roll(block, -1, axis)
    return jnp.where(speed > 0, block - lower, higher - block)


def stream(dist, velocity):
    count, width, cells = dist.shape
    padded = with_halo(dist, (("space", 1),), 1)
    lower_x = padded[:, :-2]
    higher_x = padded[:, 2:]
    cxv = velocity[0][:, None, None]
    cyv = velocity[1][:, None, None, None]
    czv = velocity[2][:, None, None, None]
    along_x = jnp.where(cxv > 0, dist - lower_x, higher_x - dist)
    grid = dist.reshape(count, width, NY, NZ)
    across = cyv * upwind_local(grid, cyv, 2) + czv * upwind_local(grid, czv, 3)
    total = cxv * along_x + across.reshape(count, width, cells)
    return dist - time_step * total


def slab_sweep(field):
    padded = with_halo(field, (("space", 1),), 1)
    beside_all = padded[:, :-2] + padded[:, 2:]
    for axis in (2, 3):
        beside_all = beside_all + jnp.roll(field, 1, axis) + jnp.roll(field, -1, axis)
    return beside_all


def smooth(local, neighbours):
    rows, width, cells = local.shape
    source = local[1:5].reshape(4, width, cells // NZ, NZ)
    field = source
    for sweep in range(SWEEPS):
        field = (source + coupling * neighbours(field)) / (1.0 + 6.0 * coupling)
    return jnp.concatenate([local[0:1], field.reshape(4, width, cells), local[5:]], 0)


def shards(dist, vel_index, relax, wall_mask, macro_inverse):
    highest = lax.Precision.HIGHEST
    count, width, cells = dist.shape
    share = cells // lax.axis_size("vel")
    velocity = velocities(vel_index)
    moment_rows, shakhov, walls = bases(velocity)
    norms = []
    owned_block = None
    for step in range(ITERS):
        read = stream(dist, velocity)
        partial_moments = jnp.dot(
            moment_rows, read.reshape(count, width * cells), precision=highest
        ).reshape(MOM, width, cells)
        totals = lax.psum(partial_moments, "vel")
        local = jnp.einsum("kj,jxc->kxc", macro_inverse, totals, precision=highest)
        updated = smooth(local, slab_sweep)
        change = lax.psum(jnp.sum((updated - totals) ** 2), "space")
        fields = jnp.concatenate([updated[0:5], updated[10:13]], 0)
        owned_block = lax.dynamic_slice_in_dim(updated, lax.axis_index("vel") * share, share, 2)
        norms.append(jnp.sqrt(change))
        flat_fields = fields.reshape(8, width * cells)
        target = jnp.dot(shakhov, flat_fields, precision=highest).reshape(count, width, cells)
        wall_fields = jnp.stack([flat_fields[0], flat_fields[4]], 0)
        wall_value = jnp.dot(walls, wall_fields, precision=highest).reshape(count, width, cells)
        dist = jnp.where(wall_mask[None] > 0, wall_value, read + relax[None] * (target - read))
    return (dist, owned_block, jnp.stack(norms))


def solution(mesh):
    return jax.shard_map(
        shards,
        mesh=mesh,
        in_specs=(P("vel", "space", None), P(None, "vel"), P("space", None), P("space", None), P()),
        out_specs=(P("vel", "space", None), P(None, "space", "vel"), P()),
        check_vma=False,
    )
```

profile of v0, /device:TPU:0, one launch (start us, length us, event | category | flops | bytes accessed | tf_op | source)
XLA Modules:
  0.0 973.2 jit_solution(570978027934620654)
XLA Ops:
  7.2 4.6 copy.217
  11.9 2.0 copy-done.4
  13.9 1.1 fusion.107
  14.9 1.9 collective-permute-start.1
  16.8 5.4 copy.208
  22.2 4.1 fusion.104
  26.9 0.9 fusion.106
  28.3 4.1 pad_maximum_fusion.4
  32.3 4.2 pad_maximum_fusion.6
  36.6 5.3 copy.210
  41.9 5.4 copy.211
  47.3 5.4 copy.214
  52.7 5.3 copy.215
  58.2 13.7 %fusion.12 = f32[128,8,1024]{2,0,1:T(8,128)} fusion(f32[128,8,1024]{2,0,1:T(8,128)} %copy-done.4, f32[128,1,1024]{2,0,1:T(8,128)} %collective-permute-done.1, f32[128,1,1024]{2,0,1:T(8,128)S(1)} %collective-permute-done, f32[128,8,1024]{2,0,1:T(8,128)} %copy.215, f32[128,8,1024]{2,0,1:T(8,128)} %copy.214, f32[128,8,1024]{2,0,1:T(8,128)} %copy.211, ...), kind=kLoop, calls=%fused_computation.16 | loop fusion | flops 18874368 | bytes 26216320 | tf_op jit(solution)/shard_map/sub | solution.py:95
  71.9 5.3 copy.218
  77.2 6.5 fusion.16
  84.1 355.4 %all-reduce.5.cloned.1.call-done = f32[13,8,1024]{2,0,1:T(8,128)} async-done(((f32[13,8,1024]{2,0,1:T(8,128)}), f32[13,8,1024]{2,0,1:T(8,128)}) %all-reduce.5.cloned.1.call-update) | async-done | bytes 426000 | tf_op jit(solution)/shard_map/psum | solution.py:128
  439.5 1.6 convolution_bitcast_fusion.1
  442.7 1.7 collective-permute-start.3
  444.5 3.1 collective-permute-done.2
  447.6 0.9 fusion.65
  450.4 1.1 collective-permute-start.5
  451.5 3.1 collective-permute-done.4
  454.5 1.0 fusion.57
  456.6 0.8 collective-permute-start.6
  457.4 1.4 collective-permute-start.7
  458.8 2.2 collective-permute-done.6
  461.3 1.0 fusion.49
  463.0 3.5 fusion.68
  466.6 5.7 bitcast_select_fusion
  472.3 5.3 copy.221
  477.6 4.1 fusion.99
  482.2 4.1 fusion.101
  486.8 2.3 fusion.102
  489.1 1.0 collective-permute-start.8
  490.1 1.0 collective-permute-start.9
  491.1 2.4 pad_maximum_fusion.8
  493.5 2.4 pad_maximum_fusion.9
  495.9 5.3 copy.222
  501.2 5.4 copy.223
  506.6 4.8 pad_maximum_fusion.10
  511.4 5.4 copy.224
  516.8 4.7 pad_maximum_fusion.11
  521.5 5.4 copy.225
  526.9 13.5 %fusion.5 = f32[128,8,1024]{2,0,1:T(8,128)} fusion(f32[128,8,1024]{2,0,1:T(8,128)} %bitcast_select_fusion, f32[128,1,1024]{2,0,1:T(8,128)S(1)} %collective-permute-done.9, f32[128,1,1024]{2,0,1:T(8,128)S(1)} %collective-permute-done.8, f32[128,8,1024]{2,0,1:T(8,128)} %copy.225, f32[128,8,1024]{2,0,1:T(8,128)} %copy.224, f32[128,8,1024]{2,0,1:T(8,128)} %copy.223, ...), kind=kLoop, calls=%fused_computation.7 | loop fusion | flops 18874368 | bytes 26216320 | tf_op jit(solution)/shard_map/sub | solution.py:95
  540.4 5.3 copy.226
  545.7 6.5 fusion.14
  553.8 351.6 %all-reduce.7.cloned.1.call-done = f32[13,8,1024]{2,0,1:T(8,128)} async-done(((f32[13,8,1024]{2,0,1:T(8,128)}), f32[13,8,1024]{2,0,1:T(8,128)}) %all-reduce.7.cloned.1.call-update) | async-done | bytes 426000 | tf_op jit(solution)/shard_map/psum | solution.py:128
  905.4 1.6 convolution_bitcast_fusion
  908.6 1.9 collective-permute-start.11
  910.7 2.7 collective-permute-done.10
  913.4 0.9 fusion.41
  915.3 0.9 collective-permute-start.12
  916.3 0.9 collective-permute-start.13
  917.2 2.9 collective-permute-done.12
  920.1 1.0 fusion.33
  922.1 1.0 collective-permute-start.14
  923.9 2.8 collective-permute-done.14
  926.7 1.0 fusion.25
  929.8 8.1 all-reduce.1
  940.2 8.2 fusion.72
  948.4 5.3 copy.229
  953.8 7.2 add_select_fusion
  961.0 4.4 copy.232
  (110 shorter events, 17.5 us)
Async XLA Ops:
  7.2 432.4 %copy-start = (f32[13,13]{1,0:T(8,128)S(1)}, f32[13,13]{1,0:T(8,128)}, u32[]{:S(2)}) copy-start(f32[13,13]{1,0:T(8,128)} %param.9) | copy-start | bytes 2032
  7.2 432.3 %all-reduce.5.cloned.1.call-start = ((), (), s32[]{:S(2)}) async-start(), calls=%async_computation | async-start | bytes 1048576 | tf_op jit(solution)/shard_map/psum | solution.py:128
  11.8 2.0 copy-start.4
  14.9 43.2 %collective-permute-start = (f32[128,1,1024]{2,0,1:T(8,128)}, f32[128,1,1024]{2,0,1:T(8,128)S(1)}, u32[]{:S(2)}, u32[]{:S(2)}) collective-permute-start(f32[128,1,1024]{2,0,1:T(8,128)} %get-tuple-element.37), channel_id=1, source_target_pairs={{0,1},{1,2},{2,3},{3,0},{4,5},{5,6},{6,7},{7,4},{8,9},{9,10},{10,1... | collective-permute-start | bytes 1572872 | tf_op jit(solution)/shard_map/ppermute | solution.py:25
  14.9 43.3 %collective-permute-start.1 = (f32[128,1,1024]{2,0,1:T(8,128)}, f32[128,1,1024]{2,0,1:T(8,128)}, u32[]{:S(2)}, u32[]{:S(2)}) collective-permute-start(f32[128,1,1024]{2,0,1:T(8,128)} %get-tuple-element.38), channel_id=1, source_target_pairs={{1,0},{2,1},{3,2},{0,3},{5,4},{6,5},{7,6},{4,7},{9,8},{10,9},{11,1... | collective-permute-start | bytes 1572872 | tf_op jit(solution)/shard_map/ppermute | solution.py:26
  22.2 4.6 copy-start.1
  26.9 1.4 copy-start.9
  77.2 6.8 copy-start.8
  83.7 821.7 %all-reduce.7.cloned.1.call-start = ((), (), s32[]{:S(2)}) async-start(), calls=%async_computation.1 | async-start | bytes 1048576 | tf_op jit(solution)/shard_map/psum | solution.py:128
  442.6 5.0 collective-permute-start.2
  442.7 4.9 collective-permute-start.3
  449.6 4.9 collective-permute-start.4
  450.4 4.2 collective-permute-start.5
  456.6 4.5 collective-permute-start.6
  457.4 3.9 collective-permute-start.7
  462.3 4.4 copy-start.7
  463.0 3.6 copy-start.3
  477.6 4.6 copy-start.2
  489.1 37.8 %collective-permute-start.8 = (f32[128,1,1024]{2,0,1:T(8,128)}, f32[128,1,1024]{2,0,1:T(8,128)S(1)}, u32[]{:S(2)}, u32[]{:S(2)}) collective-permute-start(f32[128,1,1024]{2,0,1:T(8,128)} %get-tuple-element.27), channel_id=1, source_target_pairs={{0,1},{1,2},{2,3},{3,0},{4,5},{5,6},{6,7},{7,4},{8,9},{9,10},{10,1... | collective-permute-start | bytes 1572872 | tf_op jit(solution)/shard_map/ppermute | solution.py:25
  490.1 36.8 %collective-permute-start.9 = (f32[128,1,1024]{2,0,1:T(8,128)}, f32[128,1,1024]{2,0,1:T(8,128)S(1)}, u32[]{:S(2)}, u32[]{:S(2)}) collective-permute-start(f32[128,1,1024]{2,0,1:T(8,128)} %get-tuple-element.28), channel_id=1, source_target_pairs={{1,0},{2,1},{3,2},{0,3},{5,4},{6,5},{7,6},{4,7},{9,8},{10,9},{11,1... | collective-permute-start | bytes 1572872 | tf_op jit(solution)/shard_map/ppermute | solution.py:26
  545.7 7.3 copy-start.5
  908.6 4.8 collective-permute-start.10
  908.6 4.7 collective-permute-start.11
  915.3 4.7 collective-permute-start.12
  916.3 3.8 collective-permute-start.13
  922.1 4.6 collective-permute-start.14
  923.1 3.6 collective-permute-start.15
  926.7 2.3 copy-start.6
Sparse Core Ops, SparseCore 0:
  83.9 355.6 all-reduce.4
  552.4 352.9 all-reduce.6
where the time goes:
time: 977 us; the launch traced here: 973 us
  waiting for transfers between devices  724 us (74%)
  local copies, waits for them, and re-layouts  110 us (11%)
  other arithmetic  57.9 us (6%)
  matrix products  40.9 us (4%)
  between operations  16.3 us (2%)
  starting transfers between devices  15.7 us (2%)
    psum x2, waiting for transfers between devices, shards(): totals = lax.psum(partial_moments, 'vel')  707 us
    sub x2, other arithmetic, stream(): return dist - time_step * total  27.2 us
    concatenate x4, local copies, waits for them, and re-layouts, upwind_local(): higher = jnp.roll(block, -1, axis)  21.6 us
    concatenate x4, local copies, waits for them, and re-layouts, upwind_local(): lower = jnp.roll(block, 1, axis)  21.4 us
  transfers between devices with their start and end apart: 18, of which 9 were waited for; matrix products, arithmetic and copies ran while one was open for 8% of the time, Pallas kernels for 0%

commit v1 on v0

--- a/solution.py
+++ b/solution.py
@@ -125,7 +125,7 @@
         partial_moments = jnp.dot(
             moment_rows, read.reshape(count, width * cells), precision=highest
         ).reshape(MOM, width, cells)
-        totals = lax.psum(partial_moments, "vel")
+        totals = jnp.sum(lax.all_gather(partial_moments, "vel"), axis=0)
         local = jnp.einsum("kj,jxc->kxc", macro_inverse, totals, precision=highest)
         updated = smooth(local, slab_sweep)
         change = lax.psum(jnp.sum((updated - totals) ** 2), "space")

time: 977 us -> 556 us (0.57)
  waiting for transfers between devices: 724 us -> 291 us
  other arithmetic: 57.9 us -> 70.8 us
    psum x2 -> x0, waiting for transfers between devices: 707 us -> none  [shards(): totals = lax.psum(partial_moments, 'vel')]
    all_gather x0 -> x2, waiting for transfers between devices: none -> 273 us  [shards(): totals = jnp.sum(lax.all_gather(partial_moments, 'vel'), axis=0)]
    reduce_sum x0 -> x2, other arithmetic: none -> 12.4 us  [shards(): totals = jnp.sum(lax.all_gather(partial_moments, 'vel'), axis=0)]
  transfers between devices with their start and end apart: 18 -> 18, of which waited for: 9 -> 8; matrix products, arithmetic and copies ran while one was open for 8% -> 14% of each run, Pallas kernels for 0% -> 0%
where the time goes in v1:
time: 556 us; the launch traced here: 552 us
  waiting for transfers between devices  291 us (52%)
  local copies, waits for them, and re-layouts  113 us (20%)
  other arithmetic  70.8 us (13%)
  matrix products  37.8 us (7%)
  between operations  16.2 us (3%)
  starting transfers between devices  15.4 us (3%)
  blocking collectives  7.79 us (1%)
    all_gather x2, waiting for transfers between devices, shards(): totals = jnp.sum(lax.all_gather(partial_moments, 'vel'), axis=0)  273 us
    sub x2, other arithmetic, stream(): return dist - time_step * total  27.4 us
    concatenate x4, local copies, waits for them, and re-layouts, upwind_local(): higher = jnp.roll(block, -1, axis)  21.6 us
    concatenate x4, local copies, waits for them, and re-layouts, upwind_local(): lower = jnp.roll(block, 1, axis)  21.5 us
    unnamed x20, local copies, waits for them, and re-layouts  18.1 us
    ppermute x8, waiting for transfers between devices, with_halo(): before = lax.ppermute(last, axis, up)  17.4 us
    concatenate x4, other arithmetic, upwind_local(): lower = jnp.roll(block, 1, axis)  15.5 us
    slice x8, local copies, waits for them, and re-layouts, upwind_local(): lower = jnp.roll(block, 1, axis)  14.2 us
  transfers between devices with their start and end apart: 18, of which 8 were waited for; matrix products, arithmetic and copies ran while one was open for 14% of the time, Pallas kernels for 0%

profile of v1, /device:TPU:0, one launch (start us, length us, event | category | flops | bytes accessed | tf_op | source)
XLA Modules:
  0.0 551.6 jit_solution(12788485454242428569)
XLA Ops:
  7.2 4.6 copy.225
  11.9 2.0 copy-done.4
  13.9 1.1 fusion.111
  14.9 2.2 collective-permute-start.1
  17.1 5.4 copy.216
  22.5 4.1 fusion.108
  28.6 4.1 pad_maximum_fusion.4
  32.7 4.2 pad_maximum_fusion.6
  36.9 5.4 copy.218
  42.3 5.4 copy.219
  47.7 5.4 copy.222
  53.1 5.3 copy.223
  58.6 13.7 %fusion.12 = f32[128,8,1024]{2,0,1:T(8,128)} fusion(f32[128,8,1024]{2,0,1:T(8,128)} %copy-done.4, f32[128,1,1024]{2,0,1:T(8,128)} %collective-permute-done.1, f32[128,1,1024]{2,0,1:T(8,128)S(1)} %collective-permute-done, f32[128,8,1024]{2,0,1:T(8,128)} %copy.223, f32[128,8,1024]{2,0,1:T(8,128)} %copy.222, f32[128,8,1024]{2,0,1:T(8,128)} %copy.219, ...), kind=kLoop, calls=%fused_computation.16 | loop fusion | flops 18874368 | bytes 26216320 | tf_op jit(solution)/shard_map/sub | solution.py:95
  72.3 5.3 copy.226
  77.6 5.7 %fusion.16 = f32[13,8,1024]{2,0,1:T(8,128)S(1)} fusion(f32[128,8,1024]{0,2,1:T(8,128)} %copy.226, f32[13,128]{1,0:T(8,128)S(1)} %stack.18, f32[128]{0:T(128)S(1)} %get-tuple-element.120), kind=kOutput, calls=%fused_computation.29 | convolution fusion | flops 163579520 | bytes 4627456 | tf_op jit(solution)/shard_map/dot_general | solution.py:125
  83.3 1.0 copy.227
  84.6 138.8 %all-gather.5.cloned.1.call-done = f32[416,8,1024]{2,1,0:T(8,128)} async-done(((f32[13,8,1024]{2,1,0:T(8,128)}), f32[416,8,1024]{2,1,0:T(8,128)}) %all-gather.5.cloned.1.call-update) | async-done | bytes 13631504 | tf_op jit(solution)/shard_map/all_gather | solution.py:128
  223.4 6.2 %reduce_sum.36 = f32[13,8,1024]{2,1,0:T(8,128)S(1)} reduce(f32[32,13,8,1024]{3,2,1,0:T(8,128)} %bitcast.119, f32[]{:T(128)} %constant.52.clone.1), dimensions={0}, to_apply=%region_0.1 | reduce | flops 3301376 | bytes 14057476 | tf_op jit(solution)/shard_map/reduce_sum | solution.py:128
  232.1 1.7 collective-permute-start.3
  233.9 3.1 collective-permute-done.2
  237.0 0.9 fusion.65
  239.7 1.1 collective-permute-start.5
  240.8 3.1 collective-permute-done.4
  243.9 1.0 fusion.57
  246.7 1.2 collective-permute-start.7
  247.9 2.6 collective-permute-done.6
  250.5 1.0 fusion.49
  252.2 3.5 fusion.72
  255.8 5.7 %bitcast_select_fusion = f32[128,8,1024]{2,0,1:T(8,128)} fusion(f32[16,8,8,1024]{3,2,1,0:T(8,128)S(1)} %bitcast.109, f32[128,8,1024]{2,0,1:T(8,128)S(1)} %copy-done.3, f32[8,1024,8]{1,2,0:T(8,128)S(1)} %bitcast.121, f32[8,1024]{1,0:T(8,128)S(1)} %copy-done.5, pred[8,1024]{1,0:T(8,128)(4,1)S(1)} %broadcast_compare_fusion, f32[128,8]{0,1:T(8,128)S(1)} %stack.20), kind=kOutput, calls=%fused_computation | convolution fusion | flops 104857600 | bytes 12890112 | tf_op jit(solution)/shard_map/dot_general | solution.py:136
  261.5 5.3 copy.231
  266.9 4.1 fusion.103
  271.5 4.1 fusion.105
  276.0 2.3 fusion.106
  278.3 1.0 collective-permute-start.8
  280.1 2.4 pad_maximum_fusion.8
  282.5 2.4 pad_maximum_fusion.9
  284.8 5.3 copy.232
  290.2 5.4 copy.233
  295.6 4.8 pad_maximum_fusion.10
  300.4 5.4 copy.234
  305.8 4.7 pad_maximum_fusion.11
  310.5 5.3 copy.235
  315.9 13.7 %fusion.5 = f32[128,8,1024]{2,0,1:T(8,128)} fusion(f32[128,8,1024]{2,0,1:T(8,128)} %bitcast_select_fusion, f32[128,1,1024]{2,0,1:T(8,128)} %collective-permute-done.9, f32[128,1,1024]{2,0,1:T(8,128)S(1)} %collective-permute-done.8, f32[128,8,1024]{2,0,1:T(8,128)} %copy.235, f32[128,8,1024]{2,0,1:T(8,128)} %copy.234, f32[128,8,1024]{2,0,1:T(8,128)} %copy.233, ...), kind=kLoop, calls=%fused_computation.7 | loop fusion | flops 18874368 | bytes 26216320 | tf_op jit(solution)/shard_map/sub | solution.py:95
  329.6 5.8 %copy.236 = f32[128,8,1024]{0,2,1:T(8,128)} copy(f32[128,8,1024]{2,0,1:T(8,128)} %fusion.5) | data formatting | bytes 8388608 | tf_op jit(solution)/shard_map/sub | solution.py:95
  335.4 5.7 %fusion.14 = f32[13,8,1024]{2,0,1:T(8,128)S(1)} fusion(f32[128,8,1024]{0,2,1:T(8,128)} %copy.236, f32[13,128]{1,0:T(8,128)S(1)} %stack.18, f32[128]{0:T(128)S(1)} %get-tuple-element.120), kind=kOutput, calls=%fused_computation.27 | convolution fusion | flops 163579520 | bytes 4627456 | tf_op jit(solution)/shard_map/dot_general | solution.py:125
  341.0 1.0 copy.237
  342.8 0.9 fusion.69
  343.8 134.5 %all-gather.7.cloned.1.call-done = f32[416,8,1024]{2,1,0:T(8,128)} async-done(((f32[13,8,1024]{2,1,0:T(8,128)}), f32[416,8,1024]{2,1,0:T(8,128)}) %all-gather.7.cloned.1.call-update) | async-done | bytes 13631504 | tf_op jit(solution)/shard_map/all_gather | solution.py:128
  478.3 6.2 %reduce_sum.37 = f32[13,8,1024]{2,1,0:T(8,128)S(1)} reduce(f32[32,13,8,1024]{3,2,1,0:T(8,128)} %bitcast.118, f32[]{:T(128)} %constant.52.clone.1), dimensions={0}, to_apply=%region_1.2 | reduce | flops 3301376 | bytes 14057476 | tf_op jit(solution)/shard_map/reduce_sum | solution.py:128
  486.9 1.7 collective-permute-start.11
  488.8 3.1 collective-permute-done.10
  491.9 0.9 fusion.41
  494.6 1.2 collective-permute-start.13
  495.8 2.8 collective-permute-done.12
  498.6 1.0 fusion.33
  500.6 1.0 collective-permute-start.14
  502.4 2.8 collective-permute-done.14
  505.3 1.0 fusion.25
  507.6 0.9 fusion.71
  508.5 7.8 %all-reduce.1 = (f32[]{:T(128)}, f32[]{:T(128)}) all-reduce(f32[]{:T(128)} %get-tuple-element.99, f32[]{:T(128)} %fusion.69), channel_id=1, replica_groups=mesh['vel'=32,'space'=4] {'space'}, use_global_device_ids=true, to_apply=%region_5.6 | all-reduce | flops 2 | bytes 16 | tf_op jit(solution)/shard_map/psum | solution.py:131
  518.6 8.2 %fusion.76 = f32[128,8192]{0,1:T(8,128)} fusion(f32[1,8192]{1,0:T(1,128)S(1)} %slice.499, f32[1,8192]{1,0:T(1,128)S(1)} %bitcast.124, f32[128,1]{0,1:T(1,128)S(1)} %get-tuple-element.122), kind=kOutput, calls=%fused_computation.109 | convolution fusion | flops 25182208 | bytes 4260352 | tf_op jit(solution)/shard_map/dot_general | solution.py:138
  526.8 5.3 copy.241
  532.2 7.3 %add_select_fusion = f32[128,8,1024]{2,0,1:T(8,128)S(1)} fusion(f32[128,8,1024]{2,0,1:T(8,128)} %copy.241, f32[128,8,1024]{2,0,1:T(8,128)} %fusion.5, f32[8,1024,8]{1,2,0:T(8,128)S(1)} %bitcast.120, f32[8,1024]{1,0:T(8,128)S(1)} %copy-done.5, pred[8,1024]{1,0:T(8,128)(4,1)S(1)} %broadcast_compare_fusion, f32[128,8]{0,1:T(8,128)S(1)} %stack.20), kind=kOutput, calls=%fused_computation.31 | convolution fusion | flops 104857600 | bytes 12890112 | tf_op jit(solution)/shard_map/dot_general | solution.py:136
  539.5 4.4 copy.246
  (110 shorter events, 20.7 us)
Async XLA Ops:
  7.2 222.4 %copy-start = (f32[13,13]{1,0:T(8,128)S(1)}, f32[13,13]{1,0:T(8,128)}, u32[]{:S(2)}) copy-start(f32[13,13]{1,0:T(8,128)} %param.9) | copy-start | bytes 2032
  7.2 216.2 %all-gather.5.cloned.1.call-start = ((), (), s32[]{:S(2)}) async-start(), calls=%async_computation | async-start | bytes 14057472 | tf_op jit(solution)/shard_map/all_gather | solution.py:128
  11.8 2.0 copy-start.4
  14.9 43.6 %collective-permute-start = (f32[128,1,1024]{2,0,1:T(8,128)}, f32[128,1,1024]{2,0,1:T(8,128)S(1)}, u32[]{:S(2)}, u32[]{:S(2)}) collective-permute-start(f32[128,1,1024]{2,0,1:T(8,128)} %get-tuple-element.37), channel_id=1, source_target_pairs={{0,1},{1,2},{2,3},{3,0},{4,5},{5,6},{6,7},{7,4},{8,9},{9,10},{10,1... | collective-permute-start | bytes 1572872 | tf_op jit(solution)/shard_map/ppermute | solution.py:25
  14.9 43.7 %collective-permute-start.1 = (f32[128,1,1024]{2,0,1:T(8,128)}, f32[128,1,1024]{2,0,1:T(8,128)}, u32[]{:S(2)}, u32[]{:S(2)}) collective-permute-start(f32[128,1,1024]{2,0,1:T(8,128)} %get-tuple-element.38), channel_id=1, source_target_pairs={{1,0},{2,1},{3,2},{0,3},{5,4},{6,5},{7,6},{4,7},{9,8},{10,9},{11,1... | collective-permute-start | bytes 1572872 | tf_op jit(solution)/shard_map/ppermute | solution.py:26
  22.5 4.6 copy-start.1
  27.2 1.4 copy-start.7
  77.6 7.0 %copy-start.6 = (s32[8,1024]{1,0:T(8,128)S(1)}, s32[8,1024]{1,0:T(8,128)}, u32[]{:S(2)}) copy-start(s32[8,1024]{1,0:T(8,128)} %param.8) | copy-start | bytes 98308
  84.3 394.0 %all-gather.7.cloned.1.call-start = ((), (), s32[]{:S(2)}) async-start(), calls=%async_computation.1 | async-start | bytes 14057472 | tf_op jit(solution)/shard_map/all_gather | solution.py:128
  232.0 5.0 collective-permute-start.2
  232.1 4.9 collective-permute-start.3
  238.9 4.9 collective-permute-start.4
  239.7 4.2 collective-permute-start.5
  245.9 4.6 collective-permute-start.6
  246.7 3.8 collective-permute-start.7
  251.5 4.4 copy-start.5
  252.2 3.6 copy-start.3
  266.9 4.6 copy-start.2
  278.3 37.6 %collective-permute-start.8 = (f32[128,1,1024]{2,0,1:T(8,128)}, f32[128,1,1024]{2,0,1:T(8,128)S(1)}, u32[]{:S(2)}, u32[]{:S(2)}) collective-permute-start(f32[128,1,1024]{2,0,1:T(8,128)} %get-tuple-element.27), channel_id=1, source_target_pairs={{0,1},{1,2},{2,3},{3,0},{4,5},{5,6},{6,7},{7,4},{8,9},{9,10},{10,1... | collective-permute-start | bytes 1572872 | tf_op jit(solution)/shard_map/ppermute | solution.py:25
  279.4 36.5 %collective-permute-start.9 = (f32[128,1,1024]{2,0,1:T(8,128)}, f32[128,1,1024]{2,0,1:T(8,128)}, u32[]{:S(2)}, u32[]{:S(2)}) collective-permute-start(f32[128,1,1024]{2,0,1:T(8,128)} %get-tuple-element.28), channel_id=1, source_target_pairs={{1,0},{2,1},{3,2},{0,3},{5,4},{6,5},{7,6},{4,7},{9,8},{10,9},{11,1... | collective-permute-start | bytes 1572872 | tf_op jit(solution)/shard_map/ppermute | solution.py:26
  486.9 5.0 collective-permute-start.10
  486.9 4.9 collective-permute-start.11
  493.8 4.8 collective-permute-start.12
  494.6 4.0 collective-permute-start.13
  500.6 4.7 collective-permute-start.14
  501.6 3.7 collective-permute-start.15
Sparse Core Ops, SparseCore 0:
  84.4 138.9 all-gather.4
  342.2 136.0 all-gather.6
